TPU v7x, 256 devices: a whole 4x4x8 slice. The times are simulated.
256 devices in a mesh: slab: 16 (over y, x), mode: 16 (over z, core).
Axes of the slice: x: 4, y: 4, z: 8, core: 2. Of those that a mesh axis runs over, the one named last changes fastest.
Arguments:
- tensor: bfloat16 [512, 131072], P('mode', 'slab'), may hold values from -24 to 24, as said below
- start_block: float32 [512, 128], replicated, may hold values from -6 to 6
Outputs:
- basis_rows: float32 [512, 128], P('mode')
- core_coeffs: float32 [131072, 128], P(('slab', 'mode'))
Inputs may be any that keep to these rules, and one draw needn't show every extreme that they name: `tensor`: entries of the unfolding; each is a row factor times a column factor times a bounded random term.
All inputs are finite; a program needn't handle non-finite values.
Results may differ from a plain program's by a relative error of at most 0.0029.
Values may be sent and summed in bfloat16 or wider, within the bound.
A program may use at most 64 MiB of HBM per device.

v0:
```python
import jax
import jax.numpy as jnp
from jax import lax
from jax.sharding import PartitionSpec as P

highest = lax.Precision.HIGHEST
contract_cols = (((1,), (1,)), ((), ()))
contract_rows = (((0,), (0,)), ((), ()))


def orthonormal(image_block):
    small_gram = jnp.dot(image_block.T, image_block, precision=highest)
    factor = jnp.linalg.cholesky(small_gram)
    return lax.linalg.triangular_solve(
        factor, image_block, left_side=False, lower=True, transpose_a=True
    )


def shards(tensor, start_block):
    row_count = tensor.shape[0]
    mode_index = lax.axis_index("mode")
    regrouped = lax.all_to_all(tensor, "mode", split_axis=1, concat_axis=0, tiled=True)
    local_gram = lax.dot_general(
        regrouped, regrouped, contract_cols, preferred_element_type=jnp.float32
    )
    gram_total = lax.psum(local_gram, ("slab", "mode"))
    image_block = jnp.dot(gram_total, start_block, precision=highest)
    basis_full = orthonormal(image_block)
    basis_low = basis_full.astype(jnp.bfloat16)
    basis_rows = lax.dynamic_slice_in_dim(basis_full, mode_index * row_count, row_count, 0)
    core_coeffs = lax.dot_general(
        regrouped, basis_low, contract_rows, preferred_element_type=jnp.float32
    )
    return (basis_rows, core_coeffs)


def solution(mesh):
    placed = (P("mode", "slab"), P())
    return jax.shard_map(
        shards,
        mesh=mesh,
        in_specs=placed,
        out_specs=(P("mode", None), P(("slab", "mode"), None)),
        check_vma=False,
    )
```

profile of v0, /device:TPU:2, one launch (start us, length us, event | category | flops | bytes accessed | tf_op | source)
XLA Modules:
  0.0 326.6 jit_solution(6227881989262356702)
XLA Ops:
  7.2 0.0 copy-start
  7.2 0.0 all-reduce.2.cloned.1.call-start
  7.2 1.1 copy.16
  8.4 24.3 %all_to_all.19 = bf16[32,16,512]{2,0,1:T(8,128)(2,1)S(1)} all-to-all(bf16[32,16,512]{2,0,1:T(8,128)(2,1)S(1)} %bitcast.28), channel_id=1, replica_groups=mesh['slab'=16,'mode'=16] {'mode'}, dimensions={1} | all-to-all | bytes 1048576 | tf_op jit(solution)/shard_map/all_to_all | solution.py:22
  32.7 1.5 fusion.5
  34.2 0.0 all-reduce.2.cloned.1.call-update
  34.2 257.6 %all-reduce.2.cloned.1.call-done = f32[512,512]{1,0:T(8,128)} async-done(((f32[512,512]{1,0:T(8,128)}), f32[512,512]{1,0:T(8,128)}) %all-reduce.2.cloned.1.call-update) | async-done | bytes 1048592 | tf_op jit(solution)/shard_map/psum | solution.py:26
  291.8 0.0 copy-done
  291.9 2.2 fusion.6
  294.1 0.6 fusion.7
  294.7 0.1 copy.12
  294.8 11.7 %cholesky.16 = f32[128,128]{1,0:T(8,128)S(1)} custom-call(f32[128,128]{1,0:T(8,128)S(1)} %fusion.4), custom_call_target="Cholesky" | custom-call | tf_op jit(solution)/shard_map/jit(cholesky)/cholesky | solution.py:13
  306.5 0.6 compare_reduce_fusion
  307.2 0.7 fusion.1
  307.8 9.8 %custom-call.6 = f32[1,128,128]{1,2,0:T(8,128)S(1)} custom-call(f32[1,128,128]{2,1,0:T(8,128)S(1)} %fusion.1), custom_call_target="InvertDiagBlocksLowerTriangular" | custom-call | tf_op jit(solution)/shard_map/triangular_solve | solution.py:14
  317.6 0.4 fusion.2
  318.0 0.3 convolution_bitcast_fusion
  318.3 0.6 constant_dynamic-slice_fusion
  318.9 0.8 copy.13
  (2 shorter events, 0.0 us)
Async XLA Ops:
  7.2 284.7 %copy-start = (f32[512,128]{1,0:T(8,128)S(1)}, f32[512,128]{1,0:T(8,128)}, u32[]{:S(2)}) copy-start(f32[512,128]{1,0:T(8,128)} %param.3) | copy-start | bytes 786436
  7.2 284.7 %all-reduce.2.cloned.1.call-start = ((), (), s32[]{:S(2)}) async-start(), calls=%async_computation.1 | async-start | bytes 2097152 | tf_op jit(solution)/shard_map/psum | solution.py:26
Sparse Core Ops, SparseCore 0:
  34.3 257.4 all-reduce.1
where the time goes:
time: 327 us
  waiting for transfers between devices  258 us (79%)
  blocking collectives  24.3 us (7%)
  other arithmetic  22.9 us (7%)
  between operations  14.1 us (4%)
  matrix products  4.92 us (2%)
    psum x1, waiting for transfers between devices, shards(): gram_total = lax.psum(local_gram, ('slab', 'mode'))  258 us
    all_to_all x1, blocking collectives, shards(): lax.all_to_all(tensor, 'mode', split_axis=1, concat_axis=0, tiled=True)  24.3 us
    another operation x3, other arithmetic, orthonormal(): factor = jnp.linalg.cholesky(small_gram)  12.4 us
    another operation x2, other arithmetic, orthonormal(): lax.linalg.triangular_solve(factor, image_block, left_side=False, lower=T...  10.5 us
  transfers between devices with their start and end apart: 1, of which 1 were waited for; matrix products, arithmetic and copies ran while one was open for 0% of the time, Pallas kernels for 0%

commit v1 on v0

--- a/solution.py
+++ b/solution.py
@@ -23,7 +23,8 @@
     local_gram = lax.dot_general(
         regrouped, regrouped, contract_cols, preferred_element_type=jnp.float32
     )
-    gram_total = lax.psum(local_gram, ("slab", "mode"))
+    partial = lax.psum(local_gram, "mode")
+    gram_total = lax.psum(partial, "slab")
     image_block = jnp.dot(gram_total, start_block, precision=highest)
     basis_full = orthonormal(image_block)
     basis_low = basis_full.astype(jnp.bfloat16)

time: 327 us -> 281 us (0.86)
  waiting for transfers between devices: 258 us -> 212 us
    psum x1 -> x2, waiting for transfers between devices: 258 us -> 212 us  [the longest x1 111 us: shards(): partial = lax.psum(local_gram, 'mode')]
  transfers between devices with their start and end apart: 1 -> 2, of which waited for: 1 -> 2; matrix products, arithmetic and copies ran while one was open for 0% -> 0% of each run, Pallas kernels for 0% -> 0%
where the time goes in v1:
time: 281 us
  waiting for transfers between devices  212 us (75%)
  blocking collectives  24.3 us (9%)
  other arithmetic  22.9 us (8%)
  between operations  14.1 us (5%)
  matrix products  4.92 us (2%)
    psum x1, waiting for transfers between devices, shards(): partial = lax.psum(local_gram, 'mode')  111 us
    psum x1, waiting for transfers between devices, shards(): gram_total = lax.psum(partial, 'slab')  101 us
    all_to_all x1, blocking collectives, shards(): lax.all_to_all(tensor, 'mode', split_axis=1, concat_axis=0, tiled=True)  24.3 us
    another operation x3, other arithmetic, orthonormal(): factor = jnp.linalg.cholesky(small_gram)  12.4 us
    another operation x2, other arithmetic, orthonormal(): lax.linalg.triangular_solve(factor, image_block, left_side=False, lower=T...  10.5 us
  transfers between devices with their start and end apart: 2, of which 2 were waited for; matrix products, arithmetic and copies ran while one was open for 0% of the time, Pallas kernels for 0%

profile of v1, /device:TPU:2, one launch (start us, length us, event | category | flops | bytes accessed | tf_op | source)
XLA Modules:
  0.0 280.6 jit_solution(5935104680805084658)
XLA Ops:
  7.2 0.0 copy-start
  7.2 0.0 all-reduce.3.cloned.1.call-start
  7.2 1.1 copy.16
  8.4 24.3 %all_to_all.19 = bf16[32,16,512]{2,0,1:T(8,128)(2,1)S(1)} all-to-all(bf16[32,16,512]{2,0,1:T(8,128)(2,1)S(1)} %bitcast.28), channel_id=1, replica_groups=mesh['slab'=16,'mode'=16] {'mode'}, dimensions={1} | all-to-all | bytes 1048576 | tf_op jit(solution)/shard_map/all_to_all | solution.py:22
  32.7 1.5 fusion.5
  34.2 0.0 all-reduce.3.cloned.1.call-update
  34.2 0.0 all-reduce.5.cloned.1.call-start
  34.2 111.1 %all-reduce.3.cloned.1.call-done = f32[512,512]{1,0:T(8,128)} async-done(((f32[512,512]{1,0:T(8,128)}), f32[512,512]{1,0:T(8,128)}) %all-reduce.3.cloned.1.call-update) | async-done | bytes 1048592 | tf_op jit(solution)/shard_map/psum | solution.py:26
  145.4 0.0 all-reduce.5.cloned.1.call-update
  145.4 100.5 %all-reduce.5.cloned.1.call-done = f32[512,512]{1,0:T(8,128)} async-done(((f32[512,512]{1,0:T(8,128)}), f32[512,512]{1,0:T(8,128)}) %all-reduce.5.cloned.1.call-update) | async-done | bytes 1048592 | tf_op jit(solution)/shard_map/psum | solution.py:27
  245.9 0.0 copy-done
  245.9 2.2 fusion.6
  248.1 0.6 fusion.7
  248.7 0.1 copy.12
  248.8 11.7 %cholesky.16 = f32[128,128]{1,0:T(8,128)S(1)} custom-call(f32[128,128]{1,0:T(8,128)S(1)} %fusion.4), custom_call_target="Cholesky" | custom-call | tf_op jit(solution)/shard_map/jit(cholesky)/cholesky | solution.py:13
  260.6 0.6 compare_reduce_fusion
  261.2 0.7 fusion.1
  261.9 9.8 %custom-call.6 = f32[1,128,128]{1,2,0:T(8,128)S(1)} custom-call(f32[1,128,128]{2,1,0:T(8,128)S(1)} %fusion.1), custom_call_target="InvertDiagBlocksLowerTriangular" | custom-call | tf_op jit(solution)/shard_map/triangular_solve | solution.py:14
  271.7 0.4 fusion.2
  272.1 0.3 convolution_bitcast_fusion
  272.3 0.6 constant_dynamic-slice_fusion
  272.9 0.8 copy.13
  (2 shorter events, 0.0 us)
Async XLA Ops:
  7.2 238.7 %copy-start = (f32[512,128]{1,0:T(8,128)S(1)}, f32[512,128]{1,0:T(8,128)}, u32[]{:S(2)}) copy-start(f32[512,128]{1,0:T(8,128)} %param.3) | copy-start | bytes 786436
  7.2 138.2 %all-reduce.3.cloned.1.call-start = ((), (), s32[]{:S(2)}) async-start(), calls=%async_computation.1 | async-start | bytes 2097152 | tf_op jit(solution)/shard_map/psum | solution.py:26
  34.2 211.7 %all-reduce.5.cloned.1.call-start = ((), (), s32[]{:S(2)}) async-start(), calls=%async_computation.2 | async-start | bytes 2097152 | tf_op jit(solution)/shard_map/psum | solution.py:27
Sparse Core Ops, SparseCore 0:
  34.3 110.9 all-reduce.2
  148.6 97.2 all-reduce.4
